TPU v7x, 32 devices: a whole 2x2x4 slice. The times are simulated.
32 devices in a mesh: blk: 8 (over y, x, core), feat: 4 (over z).
Axes of the slice: x: 2, y: 2, z: 4, core: 2. Of those that a mesh axis runs over, the one named last changes fastest.
Arguments:
- features: bfloat16 [24576, 512], P('blk', 'feat'), may hold values from -6 to 6
- tile_values: bfloat16 [1024, 128, 128], P('blk'), may hold values from -0.375 to 0.375
- tile_rows: int32 [1024], P('blk'), may hold values from 0 to 23, as said below
- tile_cols: int32 [1024], P('blk'), may hold values from 0 to 23, as said below
- tile_counts: int32 [64], P('blk'), may hold values from 1 to 16, as said below
- weight: bfloat16 [512, 512], replicated, may hold values from -0.25 to 0.25
- bias: float32 [512], P('feat'), may hold values from -3 to 3
Outputs:
- hidden: bfloat16 [24576, 512], P('blk', 'feat')
Inputs may be any that keep to these rules, and one draw needn't show every extreme that they name: `tile_rows`: the live slots of one node block and offset name distinct pairs of row and column tiles. `tile_cols`: paired with tile_rows slot by slot. `tile_counts`: some block and offset has all 16 slots live in every draw.
All inputs are finite; a program needn't handle non-finite values.
Results may differ from a plain program's by a relative error of at most 0.0049.
Values may be sent and summed in bfloat16 or wider, within the bound.
No kernel may reach another device: no remote copies, remote signals or barrier semaphores. Data moves between devices by JAX's collectives and lax.ppermute only.
A program may use at most 64 MiB of HBM per device.

v0:
```python
import jax
import jax.numpy as jnp
from jax import lax
from jax.sharding import PartitionSpec as P


def shifted(shard, axis, by):
    count = lax.axis_size(axis)
    return lax.ppermute(shard, axis, [(i, (i + by) % count) for i in range(count)])


def pick_tiles(current, wanted, row_tiles, tile_size):
    source = current.reshape(row_tiles, tile_size, current.shape[-1])
    return jnp.take(source, wanted, axis=0)


def add_tiles(totals, picked, offset, values_all, row_ids, tile_counts):
    row_tiles = totals.shape[0]
    slot_count = row_ids.shape[1]
    products = jnp.einsum(
        "ktj,kjf->ktf", values_all[offset], picked, preferred_element_type=jnp.float32
    )
    active = jnp.arange(slot_count) < tile_counts[offset]
    one_hot = (
        (row_ids[offset][None, :] == jnp.arange(row_tiles)[:, None]) & active[None, :]
    ).astype(jnp.float32)
    return totals + jnp.einsum("rk,ktf->rtf", one_hot, products, precision=lax.Precision.HIGHEST)


def body(features, tile_values, tile_rows, tile_cols, tile_counts, weight, bias):
    row_count, col_width = features.shape
    tile_size = tile_values.shape[-1]
    row_tiles = row_count // tile_size
    steps_all = tile_counts.shape[0]
    slot_count = tile_rows.shape[0] // steps_all
    values_all = tile_values.reshape(steps_all, slot_count, tile_size, tile_size)
    row_ids = tile_rows.reshape(steps_all, slot_count)
    col_ids = tile_cols.reshape(steps_all, slot_count)
    totals = jnp.zeros((row_tiles, tile_size, col_width), jnp.float32)
    own_picked = pick_tiles(features, col_ids[0], row_tiles, tile_size)
    totals = add_tiles(totals, own_picked, 0, values_all, row_ids, tile_counts)
    current = features
    for offset in range(1, steps_all):
        current = shifted(current, "blk", 1)
        picked = pick_tiles(current, col_ids[offset], row_tiles, tile_size)
        totals = add_tiles(totals, picked, offset, values_all, row_ids, tile_counts)
    aggregate = totals.reshape(row_count, col_width).astype(jnp.bfloat16)
    out_width = bias.shape[0]
    member = lax.axis_index("feat")
    own_cols = lax.dynamic_slice_in_dim(weight, member * out_width, out_width, 1)
    mixed = jnp.dot(
        lax.all_gather(aggregate, "feat", axis=1, tiled=True),
        own_cols,
        preferred_element_type=jnp.float32,
    )
    return jnp.maximum(mixed + bias[None, :], 0.0).astype(jnp.bfloat16)


def solution(mesh):
    in_specs = (
        P("blk", "feat"),
        P("blk", None, None),
        P("blk"),
        P("blk"),
        P("blk"),
        P(),
        P("feat"),
    )
    out_specs = P("blk", "feat")
    return jax.shard_map(body, mesh=mesh, in_specs=in_specs, out_specs=out_specs, check_vma=False)
```

profile of v0, /device:TPU:0, one launch (start us, length us, event | category | flops | bytes accessed | tf_op | source)
XLA Modules:
  0.0 183.8 jit_solution(13651544771678281297)
XLA Ops:
  9.7 1.8 gather_fusion
  15.4 4.4 %collective-permute-done = bf16[3072,128]{1,0:T(8,128)(2,1)S(1)} collective-permute-done((bf16[3072,128]{1,0:T(8,128)(2,1)}, bf16[3072,128]{1,0:T(8,128)(2,1)S(1)}, u32[]{:S(2)}, u32[]{:S(2)}) %collective-permute-start) | collective-permute-done | bytes 786464 | tf_op jit(solution)/shard_map/ppermute | solution.py:9
  22.1 10.1 %collective-permute-done.1 = bf16[3072,128]{1,0:T(8,128)(2,1)} collective-permute-done((bf16[3072,128]{1,0:T(8,128)(2,1)S(1)}, bf16[3072,128]{1,0:T(8,128)(2,1)}, u32[]{:S(2)}, u32[]{:S(2)}) %collective-permute-start.1) | collective-permute-done | bytes 786464 | tf_op jit(solution)/shard_map/ppermute | solution.py:9
  34.4 1.8 gather_fusion.1
  36.2 8.7 %collective-permute-done.2 = bf16[3072,128]{1,0:T(8,128)(2,1)} collective-permute-done((bf16[3072,128]{1,0:T(8,128)(2,1)}, bf16[3072,128]{1,0:T(8,128)(2,1)}, u32[]{:S(2)}, u32[]{:S(2)}) %collective-permute-start.2) | collective-permute-done | bytes 786464 | tf_op jit(solution)/shard_map/ppermute | solution.py:9
  44.8 2.7 %fusion.29 = f32[16,128,128]{2,1,0:T(8,128)} fusion(bf16[16,128,128]{2,1,0:T(8,128)(2,1)S(1)} %gather_fusion.1, bf16[128,128,128]{2,1,0:T(8,128)(2,1)} %param.10, pred[16]{0:T(512)(128)(4,1)S(1)} %get-tuple-element.46), kind=kOutput, calls=%fused_computation.39 | convolution fusion | flops 67371008 | bytes 2097168 | tf_op jit(solution)/shard_map/ktj,kjf->ktf/dot_general | solution.py:20
  47.5 1.7 copy.10
  49.2 2.1 %fusion.13 = f32[24,128,128]{2,0,1:T(8,128)} fusion(f32[16,128,128]{1,0,2:T(8,128)S(1)} %copy.10, s32[16]{0:T(128)S(1)} %get-tuple-element.35, pred[16]{0:T(512)(128)(4,1)S(1)} %iota_compare_fusion.14), kind=kOutput, calls=%fused_computation.23 | convolution fusion | flops 75498240 | bytes 2621520 | tf_op jit(solution)/shard_map/rk,ktf->rtf/dot_general | solution.py:27
  51.3 1.8 gather_fusion.2
  53.1 2.7 %fusion.27 = f32[16,128,128]{2,1,0:T(8,128)} fusion(bf16[16,128,128]{2,1,0:T(8,128)(2,1)S(1)} %gather_fusion.2, bf16[128,128,128]{2,1,0:T(8,128)(2,1)} %param.10, pred[16]{0:T(512)(128)(4,1)S(1)} %get-tuple-element.44), kind=kOutput, calls=%fused_computation.37 | convolution fusion | flops 67371008 | bytes 2097168 | tf_op jit(solution)/shard_map/ktj,kjf->ktf/dot_general | solution.py:20
  55.8 1.7 copy.11
  57.6 2.0 %fusion.11 = f32[24,128,128]{2,0,1:T(8,128)} fusion(f32[16,128,128]{1,0,2:T(8,128)S(1)} %copy.11, s32[16]{0:T(128)S(1)} %get-tuple-element.34, pred[16]{0:T(512)(128)(4,1)S(1)} %iota_compare_fusion.13), kind=kOutput, calls=%fused_computation.21 | convolution fusion | flops 75498240 | bytes 2621520 | tf_op jit(solution)/shard_map/rk,ktf->rtf/dot_general | solution.py:27
  59.7 1.8 gather_fusion.3
  61.5 2.7 %fusion.25 = f32[16,128,128]{2,1,0:T(8,128)} fusion(bf16[16,128,128]{2,1,0:T(8,128)(2,1)S(1)} %gather_fusion.3, bf16[128,128,128]{2,1,0:T(8,128)(2,1)} %param.10, pred[16]{0:T(512)(128)(4,1)S(1)} %get-tuple-element.42), kind=kOutput, calls=%fused_computation.35 | convolution fusion | flops 67371008 | bytes 2097168 | tf_op jit(solution)/shard_map/ktj,kjf->ktf/dot_general | solution.py:20
  64.2 1.7 copy.12
  66.0 2.1 %fusion.9 = f32[24,128,128]{2,0,1:T(8,128)} fusion(f32[16,128,128]{1,0,2:T(8,128)S(1)} %copy.12, s32[16]{0:T(128)S(1)} %get-tuple-element.33, pred[16]{0:T(512)(128)(4,1)S(1)} %iota_compare_fusion.12), kind=kOutput, calls=%fused_computation.19 | convolution fusion | flops 75498240 | bytes 2621520 | tf_op jit(solution)/shard_map/rk,ktf->rtf/dot_general | solution.py:27
  68.0 1.8 gather_fusion.4
  70.4 2.7 %fusion.23 = f32[16,128,128]{2,1,0:T(8,128)} fusion(bf16[16,128,128]{2,1,0:T(8,128)(2,1)S(1)} %gather_fusion.4, bf16[128,128,128]{2,1,0:T(8,128)(2,1)} %param.10, pred[16]{0:T(512)(128)(4,1)S(1)} %get-tuple-element.40), kind=kOutput, calls=%fused_computation.33 | convolution fusion | flops 67371008 | bytes 2097168 | tf_op jit(solution)/shard_map/ktj,kjf->ktf/dot_general | solution.py:20
  73.1 1.7 copy.13
  74.9 2.1 %fusion.7 = f32[24,128,128]{2,0,1:T(8,128)} fusion(f32[16,128,128]{1,0,2:T(8,128)S(1)} %copy.13, s32[16]{0:T(128)S(1)} %get-tuple-element.32, pred[16]{0:T(512)(128)(4,1)S(1)} %iota_compare_fusion.11), kind=kOutput, calls=%fused_computation.17 | convolution fusion | flops 75498240 | bytes 2621520 | tf_op jit(solution)/shard_map/rk,ktf->rtf/dot_general | solution.py:27
  77.0 1.8 gather_fusion.5
  78.8 2.7 %fusion.21 = f32[16,128,128]{2,1,0:T(8,128)} fusion(bf16[16,128,128]{2,1,0:T(8,128)(2,1)S(1)} %gather_fusion.5, bf16[128,128,128]{2,1,0:T(8,128)(2,1)} %param.10, pred[16]{0:T(512)(128)(4,1)S(1)} %get-tuple-element.38), kind=kOutput, calls=%fused_computation.31 | convolution fusion | flops 67371008 | bytes 2097168 | tf_op jit(solution)/shard_map/ktj,kjf->ktf/dot_general | solution.py:20
  83.2 3.6 %collective-permute-start.6 = (bf16[3072,128]{1,0:T(8,128)(2,1)}, bf16[3072,128]{1,0:T(8,128)(2,1)}, u32[]{:S(2)}, u32[]{:S(2)}) collective-permute-start(bf16[3072,128]{1,0:T(8,128)(2,1)} %collective-permute-done.5), channel_id=1, source_target_pairs={{0,4},{4,8},{8,12},{12,16},{16,20},{20,24},{24,28},{28,0},{1,5},{5... | collective-permute-start | bytes 2359304 | tf_op jit(solution)/shard_map/ppermute | solution.py:9
  86.8 2.0 %fusion.5 = f32[24,128,128]{2,0,1:T(8,128)} fusion(f32[16,128,128]{1,0,2:T(8,128)S(1)} %copy.14, s32[16]{0:T(128)S(1)} %get-tuple-element.31, pred[16]{0:T(512)(128)(4,1)S(1)} %iota_compare_fusion.10), kind=kOutput, calls=%fused_computation.15 | convolution fusion | flops 75498240 | bytes 2621520 | tf_op jit(solution)/shard_map/rk,ktf->rtf/dot_general | solution.py:27
  88.9 1.8 gather_fusion.6
  90.7 2.8 %fusion.19 = f32[16,128,128]{2,1,0:T(8,128)} fusion(bf16[16,128,128]{2,1,0:T(8,128)(2,1)S(1)} %gather_fusion.6, bf16[128,128,128]{2,1,0:T(8,128)(2,1)} %param.10, pred[16]{0:T(512)(128)(4,1)S(1)} %get-tuple-element.50), kind=kOutput, calls=%fused_computation.29 | convolution fusion | flops 67371008 | bytes 2097168 | tf_op jit(solution)/shard_map/ktj,kjf->ktf/dot_general | solution.py:20
  95.2 2.1 %fusion.3 = f32[24,128,128]{2,0,1:T(8,128)} fusion(f32[16,128,128]{1,0,2:T(8,128)S(1)} %copy.15, s32[16]{0:T(128)S(1)} %get-tuple-element.37, pred[16]{0:T(512)(128)(4,1)S(1)} %iota_compare_fusion.9), kind=kOutput, calls=%fused_computation.13 | convolution fusion | flops 75498240 | bytes 2621520 | tf_op jit(solution)/shard_map/rk,ktf->rtf/dot_general | solution.py:27
  97.3 1.8 gather_fusion.7
  99.1 2.7 %fusion.17 = f32[16,128,128]{2,1,0:T(8,128)} fusion(bf16[16,128,128]{2,1,0:T(8,128)(2,1)S(1)} %gather_fusion.7, bf16[128,128,128]{2,1,0:T(8,128)(2,1)} %param.10, pred[16]{0:T(512)(128)(4,1)S(1)} %get-tuple-element.6), kind=kOutput, calls=%fused_computation.27 | convolution fusion | flops 67371008 | bytes 2097168 | tf_op jit(solution)/shard_map/ktj,kjf->ktf/dot_general | solution.py:20
  103.5 5.0 %add_convert_fusion = bf16[24,128,128]{2,0,1:T(8,128)(2,1)S(1)} fusion(f32[24,128,128]{2,0,1:T(8,128)} %fusion.3, f32[24,128,128]{2,0,1:T(8,128)} %fusion.5, f32[24,128,128]{2,0,1:T(8,128)} %fusion.7, f32[24,128,128]{2,0,1:T(8,128)} %fusion.9, f32[24,128,128]{2,0,1:T(8,128)} %fusion.11, f32[24,128,128]{2,0,1:T(8,128)S(1)} %fusion.15, ...), kind=kOutput, calls=%fused_computation.11 | convolution fusion | flops 78643968 | bytes 12845136 | tf_op jit(solution)/shard_map/rk,ktf->rtf/dot_general | solution.py:27
  109.7 63.5 %all-gather.2.cloned.1.call-done = bf16[3072,512]{1,0:T(8,128)(2,1)} async-done(((bf16[3072,128]{1,0:T(8,128)(2,1)}), bf16[3072,512]{1,0:T(8,128)(2,1)}) %all-gather.2.cloned.1.call-update) | async-done | bytes 3145744 | tf_op jit(solution)/shard_map/all_gather | solution.py:52
  173.2 3.8 %fusion.1 = bf16[3072,128]{1,0:T(8,128)(2,1)} fusion(bf16[3072,512]{1,0:T(8,128)(2,1)} %all-gather.2.cloned.1.call-done, f32[128]{0:T(128)S(1)} %copy-done.3, bf16[512,512]{1,0:T(8,128)(2,1)S(1)} %copy-done, s32[]{:T(128)S(6)} %select_n.10), kind=kOutput, calls=%fused_computation.10 | convolution fusion | flops 403832832 | bytes 4063748 | tf_op jit(solution)/shard_map/dot_general | solution.py:51
  (46 shorter events, 18.4 us)
Async XLA Ops:
  6.5 166.7 %copy-start = (bf16[512,512]{1,0:T(8,128)(2,1)S(1)}, bf16[512,512]{1,0:T(8,128)(2,1)}, u32[]{:S(2)}) copy-start(bf16[512,512]{1,0:T(8,128)(2,1)} %param.14) | copy-start | bytes 1572868
  6.5 166.7 %all-gather.2.cloned.1.call-start = ((), (), s32[]{:S(2)}) async-start(), calls=%async_computation | async-start | bytes 3932160 | tf_op jit(solution)/shard_map/all_gather | solution.py:52
  6.5 13.2 %collective-permute-start = (bf16[3072,128]{1,0:T(8,128)(2,1)}, bf16[3072,128]{1,0:T(8,128)(2,1)S(1)}, u32[]{:S(2)}, u32[]{:S(2)}) collective-permute-start(bf16[3072,128]{1,0:T(8,128)(2,1)} %param.9), channel_id=1, source_target_pairs={{0,4},{4,8},{8,12},{12,16},{16,20},{20,24},{24,28},{28,0},{1,5},{5... | collective-permute-start | bytes 2359304 | tf_op jit(solution)/shard_map/ppermute | solution.py:9
  19.8 12.4 %copy-start.1 = (bf16[3072,128]{1,0:T(8,128)(2,1)}, bf16[3072,128]{1,0:T(8,128)(2,1)S(1)}, u32[]{:S(2)}) copy-start(bf16[3072,128]{1,0:T(8,128)(2,1)S(1)} %collective-permute-done) | copy-start | bytes 2359300
  19.8 12.4 %collective-permute-start.1 = (bf16[3072,128]{1,0:T(8,128)(2,1)S(1)}, bf16[3072,128]{1,0:T(8,128)(2,1)}, u32[]{:S(2)}, u32[]{:S(2)}) collective-permute-start(bf16[3072,128]{1,0:T(8,128)(2,1)S(1)} %collective-permute-done), channel_id=1, source_target_pairs={{0,4},{4,8},{8,12},{12,16},{16,20},{20,24},{24,28},{28,0},{1,5},{5... | collective-permute-start | bytes 2359304 | tf_op jit(solution)/shard_map/ppermute | solution.py:9
  22.1 11.3 %copy-start.2 = (s32[128]{0:T(128)S(1)}, s32[128]{0:T(128)}, u32[]{:S(2)}) copy-start(s32[128]{0:T(128)} %param.11) | copy-start | bytes 1540
  32.2 12.6 %collective-permute-start.2 = (bf16[3072,128]{1,0:T(8,128)(2,1)}, bf16[3072,128]{1,0:T(8,128)(2,1)}, u32[]{:S(2)}, u32[]{:S(2)}) collective-permute-start(bf16[3072,128]{1,0:T(8,128)(2,1)} %collective-permute-done.1), channel_id=1, source_target_pairs={{0,4},{4,8},{8,12},{12,16},{16,20},{20,24},{24,28},{28,0},{1,5},{5... | collective-permute-start | bytes 2359304 | tf_op jit(solution)/shard_map/ppermute | solution.py:9
  44.8 12.8 %collective-permute-start.3 = (bf16[3072,128]{1,0:T(8,128)(2,1)}, bf16[3072,128]{1,0:T(8,128)(2,1)}, u32[]{:S(2)}, u32[]{:S(2)}) collective-permute-start(bf16[3072,128]{1,0:T(8,128)(2,1)} %collective-permute-done.2), channel_id=1, source_target_pairs={{0,4},{4,8},{8,12},{12,16},{16,20},{20,24},{24,28},{28,0},{1,5},{5... | collective-permute-start | bytes 2359304 | tf_op jit(solution)/shard_map/ppermute | solution.py:9
  57.6 12.7 %collective-permute-start.4 = (bf16[3072,128]{1,0:T(8,128)(2,1)}, bf16[3072,128]{1,0:T(8,128)(2,1)}, u32[]{:S(2)}, u32[]{:S(2)}) collective-permute-start(bf16[3072,128]{1,0:T(8,128)(2,1)} %collective-permute-done.3), channel_id=1, source_target_pairs={{0,4},{4,8},{8,12},{12,16},{16,20},{20,24},{24,28},{28,0},{1,5},{5... | collective-permute-start | bytes 2359304 | tf_op jit(solution)/shard_map/ppermute | solution.py:9
  70.3 13.0 %collective-permute-start.5 = (bf16[3072,128]{1,0:T(8,128)(2,1)}, bf16[3072,128]{1,0:T(8,128)(2,1)}, u32[]{:S(2)}, u32[]{:S(2)}) collective-permute-start(bf16[3072,128]{1,0:T(8,128)(2,1)} %collective-permute-done.4), channel_id=1, source_target_pairs={{0,4},{4,8},{8,12},{12,16},{16,20},{20,24},{24,28},{28,0},{1,5},{5... | collective-permute-start | bytes 2359304 | tf_op jit(solution)/shard_map/ppermute | solution.py:9
  83.2 14.1 %collective-permute-start.6 = (bf16[3072,128]{1,0:T(8,128)(2,1)}, bf16[3072,128]{1,0:T(8,128)(2,1)}, u32[]{:S(2)}, u32[]{:S(2)}) collective-permute-start(bf16[3072,128]{1,0:T(8,128)(2,1)} %collective-permute-done.5), channel_id=1, source_target_pairs={{0,4},{4,8},{8,12},{12,16},{16,20},{20,24},{24,28},{28,0},{1,5},{5... | collective-permute-start | bytes 2359304 | tf_op jit(solution)/shard_map/ppermute | solution.py:9
  108.6 64.7 %copy-start.3 = (f32[128]{0:T(128)S(1)}, f32[128]{0:T(128)}, u32[]{:S(2)}) copy-start(f32[128]{0:T(128)} %param.15) | copy-start | bytes 1540
Sparse Core Ops, SparseCore 0:
  109.8 63.3 all-gather.1
where the time goes:
time: 185 us; the launch traced here: 184 us
  waiting for transfers between devices  87.2 us (47%)
  matrix products  42.9 us (23%)
  local copies, waits for them, and re-layouts  29.6 us (16%)
  between operations  13.7 us (7%)
  other arithmetic  6.13 us (3%)
  starting transfers between devices  4.29 us (2%)
    all_gather x1, waiting for transfers between devices, body(): lax.all_gather(aggregate, 'feat', axis=1, tiled=True)  63.5 us
    ppermute x7, waiting for transfers between devices, shifted(): lax.ppermute(shard, axis, [(i, (i + by) % count) for i in range(count)])  23.6 us
    dot_general x8, matrix products, add_tiles(): jnp.einsum('ktj,kjf->ktf', values_all[offset], picked, preferred_element_...  20.8 us
    dot_general x8, matrix products, add_tiles(): jnp.einsum('rk,ktf->rtf', one_hot, products, precision=lax.Precision.HIGH...  18.4 us
    gather x8, local copies, waits for them, and re-layouts, pick_tiles(): return jnp.take(source, wanted, axis=0)  14.2 us
    dot_general x8, local copies, waits for them, and re-layouts, add_tiles(): jnp.einsum('ktj,kjf->ktf', values_all[offset], picked, preferred_element_...  12.6 us
    lt x8, other arithmetic, add_tiles(): active = jnp.arange(slot_count) < tile_counts[offset]  5.05 us
    ppermute x7, starting transfers between devices, shifted(): lax.ppermute(shard, axis, [(i, (i + by) % count) for i in range(count)])  4.28 us
  transfers between devices with their start and end apart: 8, of which 5 were waited for; matrix products, arithmetic and copies ran while one was open for 34% of the time, Pallas kernels for 0%

commit v1 on v0

--- a/solution.py
+++ b/solution.py
@@ -2,6 +2,19 @@
 import jax.numpy as jnp
 from jax import lax
 from jax.sharding import PartitionSpec as P
+
+
+def collect(value, axis, dim):
+    ways = lax.axis_size(axis)
+    up = [(d, (d + 1) % ways) for d in range(ways)]
+    down = [(d, (d - 1) % ways) for d in range(ways)]
+    earlier, later = ([value], [value])
+    for _ in range(ways // 2):
+        earlier.append(lax.ppermute(earlier[-1], axis, up))
+    for _ in range((ways - 1) // 2):
+        later.append(lax.ppermute(later[-1], axis, down))
+    line = jnp.concatenate([*earlier[::-1], *later[1:]], axis=dim)
+    return jnp.roll(line, (lax.axis_index(axis) - ways // 2) * value.shape[dim], axis=dim)
 
 
 def shifted(shard, axis, by):
@@ -48,11 +61,7 @@
     out_width = bias.shape[0]
     member = lax.axis_index("feat")
     own_cols = lax.dynamic_slice_in_dim(weight, member * out_width, out_width, 1)
-    mixed = jnp.dot(
-        lax.all_gather(aggregate, "feat", axis=1, tiled=True),
-        own_cols,
-        preferred_element_type=jnp.float32,
-    )
+    mixed = jnp.dot(collect(aggregate, "feat", 1), own_cols, preferred_element_type=jnp.float32)
     return jnp.maximum(mixed + bias[None, :], 0.0).astype(jnp.bfloat16)
 
 

time: 185 us -> 164 us (0.89)
  between operations: 13.7 us -> 0.41 us
  waiting for transfers between devices: 87.2 us -> 74.3 us
  starting transfers between devices: 4.29 us -> 9.74 us
  matrix products: 42.9 us -> 41 us
    all_gather x1 -> x0, waiting for transfers between devices: 63.5 us -> none  [body(): lax.all_gather(aggregate, 'feat', axis=1, tiled=True)]
    ppermute x0 -> x3, waiting for transfers between devices: none -> 50.7 us  [the longest x2 38.2 us: collect(): earlier.append(lax.ppermute(earlier[-1], axis, up))]
    ppermute x0 -> x3, starting transfers between devices: none -> 5.45 us  [the longest x1 3.82 us: collect(): later.append(lax.ppermute(later[-1], axis, down))]
    dot_general x1, matrix products: 3.76 us -> 1.87 us  [body(): jnp.dot(collect(aggregate, 'feat', 1), own_cols, preferred_element_type=j...]
  transfers between devices with their start and end apart: 8 -> 10, of which waited for: 5 -> 7; matrix products, arithmetic and copies ran while one was open for 34% -> 39% of each run, Pallas kernels for 0% -> 0%
where the time goes in v1:
time: 164 us; the launch traced here: 162 us
  waiting for transfers between devices  74.3 us (45%)
  matrix products  41 us (25%)
  local copies, waits for them, and re-layouts  30.8 us (19%)
  starting transfers between devices  9.74 us (6%)
  other arithmetic  6.13 us (4%)
    ppermute x2, waiting for transfers between devices, collect(): earlier.append(lax.ppermute(earlier[-1], axis, up))  38.2 us
    ppermute x7, waiting for transfers between devices, shifted(): lax.ppermute(shard, axis, [(i, (i + by) % count) for i in range(count)])  23.6 us
    dot_general x8, matrix products, add_tiles(): jnp.einsum('ktj,kjf->ktf', values_all[offset], picked, preferred_element_...  20.8 us
    dot_general x8, matrix products, add_tiles(): jnp.einsum('rk,ktf->rtf', one_hot, products, precision=lax.Precision.HIGH...  18.4 us
    gather x8, local copies, waits for them, and re-layouts, pick_tiles(): return jnp.take(source, wanted, axis=0)  14.2 us
    dot_general x8, local copies, waits for them, and re-layouts, add_tiles(): jnp.einsum('ktj,kjf->ktf', values_all[offset], picked, preferred_element_...  12.6 us
    ppermute x1, waiting for transfers between devices, collect(): later.append(lax.ppermute(later[-1], axis, down))  12.5 us
    lt x8, other arithmetic, add_tiles(): active = jnp.arange(slot_count) < tile_counts[offset]  5.05 us
  transfers between devices with their start and end apart: 10, of which 7 were waited for; matrix products, arithmetic and copies ran while one was open for 39% of the time, Pallas kernels for 0%

profile of v1, /device:TPU:0, one launch (start us, length us, event | category | flops | bytes accessed | tf_op | source)
XLA Modules:
  0.0 162.4 jit_solution(13270635384834760461)
XLA Ops:
  3.1 1.8 %gather_fusion = bf16[16,128,128]{2,1,0:T(8,128)(2,1)S(1)} fusion(bf16[24,128,128]{2,1,0:T(8,128)(2,1)} %bitcast.69, s32[1024]{0:T(1024)S(1)} %pad_clamp_fusion.7), kind=kCustom, calls=%fused_computation.clone | custom fusion | bytes 1048640 | tf_op jit(solution)/shard_map/jit(_take)/gather | solution.py:27
  8.8 4.4 %collective-permute-done = bf16[3072,128]{1,0:T(8,128)(2,1)S(1)} collective-permute-done((bf16[3072,128]{1,0:T(8,128)(2,1)}, bf16[3072,128]{1,0:T(8,128)(2,1)S(1)}, u32[]{:S(2)}, u32[]{:S(2)}) %collective-permute-start) | collective-permute-done | bytes 786464 | tf_op jit(solution)/shard_map/ppermute | solution.py:22
  15.6 10.1 %collective-permute-done.1 = bf16[3072,128]{1,0:T(8,128)(2,1)} collective-permute-done((bf16[3072,128]{1,0:T(8,128)(2,1)S(1)}, bf16[3072,128]{1,0:T(8,128)(2,1)}, u32[]{:S(2)}, u32[]{:S(2)}) %collective-permute-start.1) | collective-permute-done | bytes 786464 | tf_op jit(solution)/shard_map/ppermute | solution.py:22
  27.8 1.8 %gather_fusion.1 = bf16[16,128,128]{2,1,0:T(8,128)(2,1)S(1)} fusion(bf16[24,128,128]{2,1,0:T(8,128)(2,1)} %bitcast.70, s32[1024]{0:T(1024)S(1)} %pad_clamp_fusion.6), kind=kCustom, calls=%fused_computation.1.clone | custom fusion | bytes 1048640 | tf_op jit(solution)/shard_map/jit(_take)/gather | solution.py:27
  29.6 8.7 %collective-permute-done.2 = bf16[3072,128]{1,0:T(8,128)(2,1)} collective-permute-done((bf16[3072,128]{1,0:T(8,128)(2,1)}, bf16[3072,128]{1,0:T(8,128)(2,1)}, u32[]{:S(2)}, u32[]{:S(2)}) %collective-permute-start.2) | collective-permute-done | bytes 786464 | tf_op jit(solution)/shard_map/ppermute | solution.py:22
  38.3 2.7 %fusion.30 = f32[16,128,128]{2,1,0:T(8,128)} fusion(bf16[16,128,128]{2,1,0:T(8,128)(2,1)S(1)} %gather_fusion.1, bf16[128,128,128]{2,1,0:T(8,128)(2,1)} %param.10, pred[16]{0:T(512)(128)(4,1)S(1)} %get-tuple-element.46), kind=kOutput, calls=%fused_computation.40 | convolution fusion | flops 67371008 | bytes 2097168 | tf_op jit(solution)/shard_map/ktj,kjf->ktf/dot_general | solution.py:33
  41.0 1.7 %copy.10 = f32[16,128,128]{1,0,2:T(8,128)S(1)} copy(f32[16,128,128]{2,1,0:T(8,128)} %fusion.30) | data formatting | bytes 2097152 | tf_op jit(solution)/shard_map/ktj,kjf->ktf/dot_general | solution.py:33
  42.7 2.1 %fusion.14 = f32[24,128,128]{2,0,1:T(8,128)} fusion(f32[16,128,128]{1,0,2:T(8,128)S(1)} %copy.10, s32[16]{0:T(128)S(1)} %get-tuple-element.35, pred[16]{0:T(512)(128)(4,1)S(1)} %iota_compare_fusion.14), kind=kOutput, calls=%fused_computation.24 | convolution fusion | flops 75498240 | bytes 2621520 | tf_op jit(solution)/shard_map/rk,ktf->rtf/dot_general | solution.py:40
  44.8 1.8 %gather_fusion.2 = bf16[16,128,128]{2,1,0:T(8,128)(2,1)S(1)} fusion(bf16[24,128,128]{2,1,0:T(8,128)(2,1)} %bitcast.10, s32[1024]{0:T(1024)S(1)} %pad_clamp_fusion.5), kind=kCustom, calls=%fused_computation.2.clone | custom fusion | bytes 1048640 | tf_op jit(solution)/shard_map/jit(_take)/gather | solution.py:27
  46.6 2.7 %fusion.28 = f32[16,128,128]{2,1,0:T(8,128)} fusion(bf16[16,128,128]{2,1,0:T(8,128)(2,1)S(1)} %gather_fusion.2, bf16[128,128,128]{2,1,0:T(8,128)(2,1)} %param.10, pred[16]{0:T(512)(128)(4,1)S(1)} %get-tuple-element.44), kind=kOutput, calls=%fused_computation.38 | convolution fusion | flops 67371008 | bytes 2097168 | tf_op jit(solution)/shard_map/ktj,kjf->ktf/dot_general | solution.py:33
  51.1 2.0 %fusion.12 = f32[24,128,128]{2,0,1:T(8,128)} fusion(f32[16,128,128]{1,0,2:T(8,128)S(1)} %copy.11, s32[16]{0:T(128)S(1)} %get-tuple-element.34, pred[16]{0:T(512)(128)(4,1)S(1)} %iota_compare_fusion.13), kind=kOutput, calls=%fused_computation.22 | convolution fusion | flops 75498240 | bytes 2621520 | tf_op jit(solution)/shard_map/rk,ktf->rtf/dot_general | solution.py:40
  53.2 1.8 %gather_fusion.3 = bf16[16,128,128]{2,1,0:T(8,128)(2,1)S(1)} fusion(bf16[24,128,128]{2,1,0:T(8,128)(2,1)} %bitcast.14, s32[1024]{0:T(1024)S(1)} %pad_clamp_fusion.4), kind=kCustom, calls=%fused_computation.3.clone | custom fusion | bytes 1048640 | tf_op jit(solution)/shard_map/jit(_take)/gather | solution.py:27
  54.9 2.7 %fusion.26 = f32[16,128,128]{2,1,0:T(8,128)} fusion(bf16[16,128,128]{2,1,0:T(8,128)(2,1)S(1)} %gather_fusion.3, bf16[128,128,128]{2,1,0:T(8,128)(2,1)} %param.10, pred[16]{0:T(512)(128)(4,1)S(1)} %get-tuple-element.42), kind=kOutput, calls=%fused_computation.36 | convolution fusion | flops 67371008 | bytes 2097168 | tf_op jit(solution)/shard_map/ktj,kjf->ktf/dot_general | solution.py:33
  59.4 2.1 %fusion.10 = f32[24,128,128]{2,0,1:T(8,128)} fusion(f32[16,128,128]{1,0,2:T(8,128)S(1)} %copy.12, s32[16]{0:T(128)S(1)} %get-tuple-element.33, pred[16]{0:T(512)(128)(4,1)S(1)} %iota_compare_fusion.12), kind=kOutput, calls=%fused_computation.20 | convolution fusion | flops 75498240 | bytes 2621520 | tf_op jit(solution)/shard_map/rk,ktf->rtf/dot_general | solution.py:40
  61.5 1.8 %gather_fusion.4 = bf16[16,128,128]{2,1,0:T(8,128)(2,1)S(1)} fusion(bf16[24,128,128]{2,1,0:T(8,128)(2,1)} %bitcast.18, s32[1024]{0:T(1024)S(1)} %pad_clamp_fusion.3), kind=kCustom, calls=%fused_computation.4.clone | custom fusion | bytes 1048640 | tf_op jit(solution)/shard_map/jit(_take)/gather | solution.py:27
  63.9 2.7 %fusion.24 = f32[16,128,128]{2,1,0:T(8,128)} fusion(bf16[16,128,128]{2,1,0:T(8,128)(2,1)S(1)} %gather_fusion.4, bf16[128,128,128]{2,1,0:T(8,128)(2,1)} %param.10, pred[16]{0:T(512)(128)(4,1)S(1)} %get-tuple-element.40), kind=kOutput, calls=%fused_computation.34 | convolution fusion | flops 67371008 | bytes 2097168 | tf_op jit(solution)/shard_map/ktj,kjf->ktf/dot_general | solution.py:33
  68.3 2.1 %fusion.8 = f32[24,128,128]{2,0,1:T(8,128)} fusion(f32[16,128,128]{1,0,2:T(8,128)S(1)} %copy.13, s32[16]{0:T(128)S(1)} %get-tuple-element.32, pred[16]{0:T(512)(128)(4,1)S(1)} %iota_compare_fusion.11), kind=kOutput, calls=%fused_computation.18 | convolution fusion | flops 75498240 | bytes 2621520 | tf_op jit(solution)/shard_map/rk,ktf->rtf/dot_general | solution.py:40
  70.4 1.8 %gather_fusion.5 = bf16[16,128,128]{2,1,0:T(8,128)(2,1)S(1)} fusion(bf16[24,128,128]{2,1,0:T(8,128)(2,1)} %bitcast.22, s32[1024]{0:T(1024)S(1)} %pad_clamp_fusion.2), kind=kCustom, calls=%fused_computation.5.clone | custom fusion | bytes 1048640 | tf_op jit(solution)/shard_map/jit(_take)/gather | solution.py:27
  72.2 2.7 %fusion.22 = f32[16,128,128]{2,1,0:T(8,128)} fusion(bf16[16,128,128]{2,1,0:T(8,128)(2,1)S(1)} %gather_fusion.5, bf16[128,128,128]{2,1,0:T(8,128)(2,1)} %param.10, pred[16]{0:T(512)(128)(4,1)S(1)} %get-tuple-element.38), kind=kOutput, calls=%fused_computation.32 | convolution fusion | flops 67371008 | bytes 2097168 | tf_op jit(solution)/shard_map/ktj,kjf->ktf/dot_general | solution.py:33
  76.7 3.6 %collective-permute-start.6 = (bf16[3072,128]{1,0:T(8,128)(2,1)}, bf16[3072,128]{1,0:T(8,128)(2,1)}, u32[]{:S(2)}, u32[]{:S(2)}) collective-permute-start(bf16[3072,128]{1,0:T(8,128)(2,1)} %collective-permute-done.5), channel_id=1, source_target_pairs={{0,4},{4,8},{8,12},{12,16},{16,20},{20,24},{24,28},{28,0},{1,5},{5... | collective-permute-start | bytes 2359304 | tf_op jit(solution)/shard_map/ppermute | solution.py:22
  80.3 2.0 %fusion.6 = f32[24,128,128]{2,0,1:T(8,128)} fusion(f32[16,128,128]{1,0,2:T(8,128)S(1)} %copy.14, s32[16]{0:T(128)S(1)} %get-tuple-element.31, pred[16]{0:T(512)(128)(4,1)S(1)} %iota_compare_fusion.10), kind=kOutput, calls=%fused_computation.16 | convolution fusion | flops 75498240 | bytes 2621520 | tf_op jit(solution)/shard_map/rk,ktf->rtf/dot_general | solution.py:40
  82.3 1.8 %gather_fusion.6 = bf16[16,128,128]{2,1,0:T(8,128)(2,1)S(1)} fusion(bf16[24,128,128]{2,1,0:T(8,128)(2,1)} %bitcast.26, s32[1024]{0:T(1024)S(1)} %pad_clamp_fusion.1), kind=kCustom, calls=%fused_computation.6.clone | custom fusion | bytes 1048640 | tf_op jit(solution)/shard_map/jit(_take)/gather | solution.py:27
  84.1 2.8 %fusion.20 = f32[16,128,128]{2,1,0:T(8,128)} fusion(bf16[16,128,128]{2,1,0:T(8,128)(2,1)S(1)} %gather_fusion.6, bf16[128,128,128]{2,1,0:T(8,128)(2,1)} %param.10, pred[16]{0:T(512)(128)(4,1)S(1)} %get-tuple-element.50), kind=kOutput, calls=%fused_computation.30 | convolution fusion | flops 67371008 | bytes 2097168 | tf_op jit(solution)/shard_map/ktj,kjf->ktf/dot_general | solution.py:33
  88.6 2.1 %fusion.4 = f32[24,128,128]{2,0,1:T(8,128)} fusion(f32[16,128,128]{1,0,2:T(8,128)S(1)} %copy.15, s32[16]{0:T(128)S(1)} %get-tuple-element.37, pred[16]{0:T(512)(128)(4,1)S(1)} %iota_compare_fusion.9), kind=kOutput, calls=%fused_computation.14 | convolution fusion | flops 75498240 | bytes 2621520 | tf_op jit(solution)/shard_map/rk,ktf->rtf/dot_general | solution.py:40
  90.8 1.8 %gather_fusion.7 = bf16[16,128,128]{2,1,0:T(8,128)(2,1)S(1)} fusion(bf16[24,128,128]{2,1,0:T(8,128)(2,1)} %bitcast.30, s32[1024]{0:T(1024)S(1)} %pad_clamp_fusion), kind=kCustom, calls=%fused_computation.7.clone | custom fusion | bytes 1048640 | tf_op jit(solution)/shard_map/jit(_take)/gather | solution.py:27
  92.6 2.7 %fusion.18 = f32[16,128,128]{2,1,0:T(8,128)} fusion(bf16[16,128,128]{2,1,0:T(8,128)(2,1)S(1)} %gather_fusion.7, bf16[128,128,128]{2,1,0:T(8,128)(2,1)} %param.10, pred[16]{0:T(512)(128)(4,1)S(1)} %get-tuple-element.6), kind=kOutput, calls=%fused_computation.28 | convolution fusion | flops 67371008 | bytes 2097168 | tf_op jit(solution)/shard_map/ktj,kjf->ktf/dot_general | solution.py:33
  97.0 5.0 %add_convert_fusion = bf16[24,128,128]{2,0,1:T(8,128)(2,1)S(1)} fusion(f32[24,128,128]{2,0,1:T(8,128)} %fusion.4, f32[24,128,128]{2,0,1:T(8,128)} %fusion.6, f32[24,128,128]{2,0,1:T(8,128)} %fusion.8, f32[24,128,128]{2,0,1:T(8,128)} %fusion.10, f32[24,128,128]{2,0,1:T(8,128)} %fusion.12, f32[24,128,128]{2,0,1:T(8,128)S(1)} %fusion.16, ...), kind=kOutput, calls=%fused_computation.12 | convolution fusion | flops 78643968 | bytes 12845136 | tf_op jit(solution)/shard_map/rk,ktf->rtf/dot_general | solution.py:40
  103.8 19.8 %collective-permute-done.7 = bf16[3072,128]{1,0:T(8,128)(2,1)S(1)} collective-permute-done((bf16[3072,128]{1,0:T(8,128)(2,1)S(1)}, bf16[3072,128]{1,0:T(8,128)(2,1)S(1)}, u32[]{:S(2)}, u32[]{:S(2)}) %collective-permute-start.7) | collective-permute-done | bytes 786464 | tf_op jit(solution)/shard_map/ppermute | solution.py:13
  123.6 3.8 %collective-permute-start.9 = (bf16[3072,128]{1,0:T(8,128)(2,1)S(1)}, bf16[3072,128]{1,0:T(8,128)(2,1)S(1)}, u32[]{:S(2)}, u32[]{:S(2)}) collective-permute-start(bf16[3072,128]{1,0:T(8,128)(2,1)S(1)} %bitcast.66), channel_id=1, source_target_pairs={{0,3},{1,0},{2,1},{3,2},{4,7},{5,4},{6,5},{7,6},{8,11},{9,8},{10,9... | collective-permute-start | bytes 2359304 | tf_op jit(solution)/shard_map/ppermute | solution.py:15
  127.4 18.5 %collective-permute-done.8 = bf16[3072,128]{1,0:T(8,128)(2,1)S(1)} collective-permute-done((bf16[3072,128]{1,0:T(8,128)(2,1)S(1)}, bf16[3072,128]{1,0:T(8,128)(2,1)S(1)}, u32[]{:S(2)}, u32[]{:S(2)}) %collective-permute-start.8) | collective-permute-done | bytes 786464 | tf_op jit(solution)/shard_map/ppermute | solution.py:13
  146.7 12.5 %collective-permute-done.9 = bf16[3072,128]{1,0:T(8,128)(2,1)S(1)} collective-permute-done((bf16[3072,128]{1,0:T(8,128)(2,1)S(1)}, bf16[3072,128]{1,0:T(8,128)(2,1)S(1)}, u32[]{:S(2)}, u32[]{:S(2)}) %collective-permute-start.9) | collective-permute-done | bytes 786464 | tf_op jit(solution)/shard_map/ppermute | solution.py:15
  160.6 1.9 %fusion.1 = bf16[3072,128]{1,0:T(8,128)(2,1)} fusion(bf16[3072,1024]{1,0:T(8,128)(2,1)S(1)} %constant_dynamic-update-slice_fusion, s32[]{:T(128)S(6)} %select_n.24, f32[128]{0:T(128)S(1)} %copy-done.3, bf16[512,512]{1,0:T(8,128)(2,1)S(1)} %copy-done, s32[]{:T(128)S(6)} %select_n.25), kind=kOutput, calls=%fused_computation.10 | convolution fusion | flops 403832832 | bytes 4063752 | tf_op jit(solution)/shard_map/dot_general | solution.py:64
  (57 shorter events, 26.4 us)
Async XLA Ops:
  0.0 160.5 %copy-start = (bf16[512,512]{1,0:T(8,128)(2,1)S(1)}, bf16[512,512]{1,0:T(8,128)(2,1)}, u32[]{:S(2)}) copy-start(bf16[512,512]{1,0:T(8,128)(2,1)} %param.14) | copy-start | bytes 1572868
  0.0 26.8 %copy-start.2 = (s32[128]{0:T(128)S(1)}, s32[128]{0:T(128)}, u32[]{:S(2)}) copy-start(s32[128]{0:T(128)} %param.11) | copy-start | bytes 1540
  0.0 13.2 %collective-permute-start = (bf16[3072,128]{1,0:T(8,128)(2,1)}, bf16[3072,128]{1,0:T(8,128)(2,1)S(1)}, u32[]{:S(2)}, u32[]{:S(2)}) collective-permute-start(bf16[3072,128]{1,0:T(8,128)(2,1)} %param.9), channel_id=1, source_target_pairs={{0,4},{4,8},{8,12},{12,16},{16,20},{20,24},{24,28},{28,0},{1,5},{5... | collective-permute-start | bytes 2359304 | tf_op jit(solution)/shard_map/ppermute | solution.py:22
  13.2 12.4 %copy-start.1 = (bf16[3072,128]{1,0:T(8,128)(2,1)}, bf16[3072,128]{1,0:T(8,128)(2,1)S(1)}, u32[]{:S(2)}) copy-start(bf16[3072,128]{1,0:T(8,128)(2,1)S(1)} %collective-permute-done) | copy-start | bytes 2359300
  13.2 12.4 %collective-permute-start.1 = (bf16[3072,128]{1,0:T(8,128)(2,1)S(1)}, bf16[3072,128]{1,0:T(8,128)(2,1)}, u32[]{:S(2)}, u32[]{:S(2)}) collective-permute-start(bf16[3072,128]{1,0:T(8,128)(2,1)S(1)} %collective-permute-done), channel_id=1, source_target_pairs={{0,4},{4,8},{8,12},{12,16},{16,20},{20,24},{24,28},{28,0},{1,5},{5... | collective-permute-start | bytes 2359304 | tf_op jit(solution)/shard_map/ppermute | solution.py:22
  25.6 12.6 %collective-permute-start.2 = (bf16[3072,128]{1,0:T(8,128)(2,1)}, bf16[3072,128]{1,0:T(8,128)(2,1)}, u32[]{:S(2)}, u32[]{:S(2)}) collective-permute-start(bf16[3072,128]{1,0:T(8,128)(2,1)} %collective-permute-done.1), channel_id=1, source_target_pairs={{0,4},{4,8},{8,12},{12,16},{16,20},{20,24},{24,28},{28,0},{1,5},{5... | collective-permute-start | bytes 2359304 | tf_op jit(solution)/shard_map/ppermute | solution.py:22
  38.3 12.8 %collective-permute-start.3 = (bf16[3072,128]{1,0:T(8,128)(2,1)}, bf16[3072,128]{1,0:T(8,128)(2,1)}, u32[]{:S(2)}, u32[]{:S(2)}) collective-permute-start(bf16[3072,128]{1,0:T(8,128)(2,1)} %collective-permute-done.2), channel_id=1, source_target_pairs={{0,4},{4,8},{8,12},{12,16},{16,20},{20,24},{24,28},{28,0},{1,5},{5... | collective-permute-start | bytes 2359304 | tf_op jit(solution)/shard_map/ppermute | solution.py:22
  51.0 12.7 %collective-permute-start.4 = (bf16[3072,128]{1,0:T(8,128)(2,1)}, bf16[3072,128]{1,0:T(8,128)(2,1)}, u32[]{:S(2)}, u32[]{:S(2)}) collective-permute-start(bf16[3072,128]{1,0:T(8,128)(2,1)} %collective-permute-done.3), channel_id=1, source_target_pairs={{0,4},{4,8},{8,12},{12,16},{16,20},{20,24},{24,28},{28,0},{1,5},{5... | collective-permute-start | bytes 2359304 | tf_op jit(solution)/shard_map/ppermute | solution.py:22
  63.7 13.0 %collective-permute-start.5 = (bf16[3072,128]{1,0:T(8,128)(2,1)}, bf16[3072,128]{1,0:T(8,128)(2,1)}, u32[]{:S(2)}, u32[]{:S(2)}) collective-permute-start(bf16[3072,128]{1,0:T(8,128)(2,1)} %collective-permute-done.4), channel_id=1, source_target_pairs={{0,4},{4,8},{8,12},{12,16},{16,20},{20,24},{24,28},{28,0},{1,5},{5... | collective-permute-start | bytes 2359304 | tf_op jit(solution)/shard_map/ppermute | solution.py:22
  76.7 14.1 %collective-permute-start.6 = (bf16[3072,128]{1,0:T(8,128)(2,1)}, bf16[3072,128]{1,0:T(8,128)(2,1)}, u32[]{:S(2)}, u32[]{:S(2)}) collective-permute-start(bf16[3072,128]{1,0:T(8,128)(2,1)} %collective-permute-done.5), channel_id=1, source_target_pairs={{0,4},{4,8},{8,12},{12,16},{16,20},{20,24},{24,28},{28,0},{1,5},{5... | collective-permute-start | bytes 2359304 | tf_op jit(solution)/shard_map/ppermute | solution.py:22
  102.2 21.4 %collective-permute-start.7 = (bf16[3072,128]{1,0:T(8,128)(2,1)S(1)}, bf16[3072,128]{1,0:T(8,128)(2,1)S(1)}, u32[]{:S(2)}, u32[]{:S(2)}) collective-permute-start(bf16[3072,128]{1,0:T(8,128)(2,1)S(1)} %bitcast.65), channel_id=1, source_target_pairs={{0,1},{1,2},{2,3},{3,0},{4,5},{5,6},{6,7},{7,4},{8,9},{9,10},{10,1... | collective-permute-start | bytes 2359304 | tf_op jit(solution)/shard_map/ppermute | solution.py:13
  123.6 22.3 %collective-permute-start.8 = (bf16[3072,128]{1,0:T(8,128)(2,1)S(1)}, bf16[3072,128]{1,0:T(8,128)(2,1)S(1)}, u32[]{:S(2)}, u32[]{:S(2)}) collective-permute-start(bf16[3072,128]{1,0:T(8,128)(2,1)S(1)} %collective-permute-done.7), channel_id=1, source_target_pairs={{0,1},{1,2},{2,3},{3,0},{4,5},{5,6},{6,7},{7,4},{8,9},{9,10},{10,1... | collective-permute-start | bytes 2359304 | tf_op jit(solution)/shard_map/ppermute | solution.py:13
  123.6 35.6 %collective-permute-start.9 = (bf16[3072,128]{1,0:T(8,128)(2,1)S(1)}, bf16[3072,128]{1,0:T(8,128)(2,1)S(1)}, u32[]{:S(2)}, u32[]{:S(2)}) collective-permute-start(bf16[3072,128]{1,0:T(8,128)(2,1)S(1)} %bitcast.66), channel_id=1, source_target_pairs={{0,3},{1,0},{2,1},{3,2},{4,7},{5,4},{6,5},{7,6},{8,11},{9,8},{10,9... | collective-permute-start | bytes 2359304 | tf_op jit(solution)/shard_map/ppermute | solution.py:15
  146.7 13.9 %copy-start.3 = (f32[128]{0:T(128)S(1)}, f32[128]{0:T(128)}, u32[]{:S(2)}) copy-start(f32[128]{0:T(128)} %param.15) | copy-start | bytes 1540
